TPU v7x, 32 devices: a whole 2x2x4 slice. The times are simulated.
32 devices in a mesh: layer: 4 (over y, core), front: 8 (over z, x).
Axes of the slice: x: 2, y: 2, z: 4, core: 2. Of those that a mesh axis runs over, the one named last changes fastest.
Arguments:
- child_rhs: bfloat16 [4, 2, 48, 8192], P('layer', None, None, 'front'), may hold values from -6 to 6
- parent_rhs: bfloat16 [4, 2, 48, 4096], P('layer', None, None, 'front'), may hold values from -6 to 6
- root_rhs: bfloat16 [4, 2, 48, 4096], P('layer', None, None, 'front'), may hold values from -6 to 6
- child_inverse: bfloat16 [4, 2048, 8192], P('layer', None, 'front'), as said below
- child_update: bfloat16 [4, 8192, 2048], P('layer', 'front'), may hold values from -0.125 to 0.125
- parent_inverse: bfloat16 [4, 2048, 4096], P('layer', None, 'front'), as said below
- parent_update: bfloat16 [4, 4096, 3072], P('layer', 'front'), may hold values from -0.125 to 0.125
- root_inverse: bfloat16 [4, 4096, 4096], P('layer', None, 'front'), as said below
- coupling: float32 [4, 4096], P('layer', 'front'), may hold values from 0.25 to 1
- child_map: int32 [4, 2048], replicated, may hold values from 0 to 6143, as said below
- parent_map: int32 [2, 3072], replicated, may hold values from 0 to 4095, as said below
Outputs:
- solution: bfloat16 [4, 2, 48, 4096], P('layer', None, None, 'front')
Inputs may be any that keep to these rules, and one draw needn't show every extreme that they name: `child_map`: each row holds 2048 distinct entries; values below 2048 name rows of the parent front's separator, the others name row value - 2048 of the top separator. `parent_map`: each row holds 3072 distinct rows of the top separator. `child_inverse`: each group's matrix, read as rows k and columns f * 2048 + j, is zero where k > j. `parent_inverse`: each group's matrix, read as rows k and columns f * 2048 + j, is zero where k > j. `root_inverse`: each group's matrix is zero below its diagonal.
All inputs are finite; a program needn't handle non-finite values.
Results may differ from a plain program's by a relative error of at most 0.02.
Values may be sent and summed in bfloat16 or wider, within the bound.
No kernel may reach another device: no remote copies, remote signals or barrier semaphores. Data moves between devices by JAX's collectives and lax.ppermute only.
A program may use at most 64 MiB of HBM per device.

v0:
```python
import jax
import jax.numpy as jnp
from jax import lax
from jax.sharding import PartitionSpec as P

S0 = 4096


def partner_2(value, axis, apart):
    mask = 2**apart
    pairs = [(source, source ^ mask) for source in range(lax.axis_size(axis))]
    return lax.ppermute(value, axis, pairs)


def shifted(value, axis, steps):
    count = lax.axis_size(axis)
    first, last = (max(0, -steps), min(count, count - steps))
    return lax.ppermute(value, axis, [(source, source + steps) for source in range(first, last)])


def collect(shard, share_count, level_id):
    front_index = lax.axis_index("front")
    bit_count = share_count.bit_length() - 1
    joined = shard
    for bit_pos in range(bit_count):
        if level_id == 2:
            partner = partner_2(joined, "front", bit_pos)
        else:
            partner = partner_2(joined, "front", bit_pos)
        high_bit = front_index >> bit_pos & 1 == 1
        first_piece = jnp.where(high_bit, partner, joined)
        second_piece = jnp.where(high_bit, joined, partner)
        joined = jnp.concatenate([first_piece, second_piece], 1)
    return joined


def parent_updates(own_parent, parent_shares):
    front_index = lax.axis_index("front")
    buffer = lax.optimization_barrier(own_parent.astype(jnp.bfloat16)).astype(jnp.float32)
    bit_count = parent_shares.bit_length() - 1
    for bit_pos in reversed(range(bit_count)):
        half_width = buffer.shape[1] // 2
        lower_cols = buffer[:, :half_width]
        upper_cols = buffer[:, half_width:]
        upper_side = front_index >> bit_pos & 1 == 1
        sending = jnp.where(upper_side, lower_cols, upper_cols)
        partner = partner_2(sending.astype(jnp.bfloat16), "front", bit_pos).astype(sending.dtype)
        buffer = jnp.where(upper_side, upper_cols, lower_cols) + partner
    return buffer


def lower_levels(
    child_rhs,
    parent_rhs,
    child_inverse,
    child_update,
    parent_inverse,
    parent_update,
    child_map,
    parent_map,
):
    devices = lax.axis_size("front")
    front_index = lax.axis_index("front")
    child_shares = devices // 4
    parent_shares = devices // 2
    row_count = child_rhs.shape[0]
    parent_size = parent_inverse.shape[0]
    child_full = collect(child_rhs, child_shares, 2)
    child_solved = jnp.dot(child_full, child_inverse, preferred_element_type=jnp.float32).astype(
        jnp.bfloat16
    )
    child_terms = jnp.dot(child_solved, child_update, preferred_element_type=jnp.float32)
    child_front = front_index // child_shares
    targets = child_map[child_front]
    to_parent = jnp.where(targets < parent_size, targets, parent_size)
    to_root = jnp.where(targets >= parent_size, targets - parent_size, S0)
    own_parent = (
        jnp.zeros((row_count, parent_size), jnp.float32)
        .at[:, to_parent]
        .add(child_terms, mode="drop")
    )
    root_terms = (
        jnp.zeros((row_count, S0), jnp.float32).at[:, to_root].add(child_terms, mode="drop")
    )
    summed = parent_updates(own_parent, parent_shares)
    parent_now = (parent_rhs.astype(jnp.float32) - summed).astype(jnp.bfloat16)
    parent_full = collect(parent_now, parent_shares, 1)
    parent_solved = jnp.dot(parent_full, parent_inverse, preferred_element_type=jnp.float32).astype(
        jnp.bfloat16
    )
    parent_terms = jnp.dot(parent_solved, parent_update, preferred_element_type=jnp.float32)
    parent_targets = parent_map[front_index // parent_shares]
    return root_terms.at[:, parent_targets].add(parent_terms)


def root_level(root_terms, root_rhs, incoming, root_inverse, coupling):
    front_index = lax.axis_index("front")
    share_width = root_rhs.shape[1]
    own_cols = lax.dynamic_slice_in_dim(root_terms, front_index * share_width, share_width, 1)
    own_cols = own_cols + incoming.astype(jnp.float32) - root_rhs.astype(jnp.float32)
    root_total = lax.dynamic_update_slice_in_dim(root_terms, own_cols, front_index * share_width, 1)
    summed = lax.psum(root_total.astype(jnp.bfloat16), "front").astype(jnp.float32)
    root_now = (-summed).astype(jnp.bfloat16)
    root_solved = jnp.dot(root_now, root_inverse, preferred_element_type=jnp.float32)
    return (
        root_solved.astype(jnp.bfloat16),
        (coupling[None, :] * root_solved).astype(jnp.bfloat16),
    )


def body(
    child_rhs,
    parent_rhs,
    root_rhs,
    child_inverse,
    child_update,
    parent_inverse,
    parent_update,
    root_inverse,
    coupling,
    child_map,
    parent_map,
):
    row_count = child_rhs.shape[2]
    stacked_terms = lower_levels(
        child_rhs[0].reshape(2 * row_count, child_rhs.shape[3]),
        parent_rhs[0].reshape(2 * row_count, parent_rhs.shape[3]),
        child_inverse[0],
        child_update[0],
        parent_inverse[0],
        parent_update[0],
        child_map,
        parent_map,
    )
    first_terms = stacked_terms[:row_count]
    second_terms = stacked_terms[row_count:]
    silent = jnp.zeros_like(root_rhs[0, 0])
    first_sol, outgoing = root_level(
        first_terms, root_rhs[0, 0], silent, root_inverse[0], coupling[0]
    )
    incoming = shifted(outgoing, "layer", 1)
    second_sol, leftover = root_level(
        second_terms, root_rhs[0, 1], incoming, root_inverse[0], coupling[0]
    )
    return jnp.stack([first_sol, second_sol], axis=0)[None]


def solution(mesh):
    placed = (
        P("layer", None, None, "front"),
        P("layer", None, None, "front"),
        P("layer", None, None, "front"),
        P("layer", None, "front"),
        P("layer", "front", None),
        P("layer", None, "front"),
        P("layer", "front", None),
        P("layer", None, "front"),
        P("layer", "front"),
        P(),
        P(),
    )
    return jax.shard_map(
        body, mesh=mesh, in_specs=placed, out_specs=P("layer", None, None, "front"), check_vma=False
    )
```

profile of v0, /device:TPU:0, one launch (start us, length us, event | category | flops | bytes accessed | tf_op | source)
XLA Modules:
  0.0 282.1 jit_solution(15062157132926569334)
XLA Ops:
  6.5 3.0 %collective-permute-start = (bf16[96,1024]{1,0:T(8,128)(2,1)}, bf16[96,1024]{1,0:T(8,128)(2,1)}, u32[]{:S(2)}, u32[]{:S(2)}) collective-permute-start(bf16[96,1024]{1,0:T(8,128)(2,1)} %bitcast.67), channel_id=1, source_target_pairs={{0,1},{1,0},{2,3},{3,2},{4,5},{5,4},{6,7},{7,6},{8,9},{9,8},{10,11... | collective-permute-start | bytes 589832 | tf_op jit(solution)/shard_map/ppermute | solution.py:12
  9.5 1.4 compare_select_fusion.1
  10.9 3.8 %collective-permute-done = bf16[96,1024]{1,0:T(8,128)(2,1)} collective-permute-done((bf16[96,1024]{1,0:T(8,128)(2,1)}, bf16[96,1024]{1,0:T(8,128)(2,1)}, u32[]{:S(2)}, u32[]{:S(2)}) %collective-permute-start) | collective-permute-done | bytes 196640 | tf_op jit(solution)/shard_map/ppermute | solution.py:12
  14.7 1.1 broadcast_select_fusion.3
  15.8 5.8 %fusion.9 = f32[2048,96]{0,1:T(8,128)} fusion(bf16[1,1024,2048]{2,1,0:T(8,128)(2,1)} %param.15, bf16[1,2048,1024]{2,1,0:T(8,128)(2,1)} %param.14, bf16[96,1024]{1,0:T(8,128)(2,1)S(1)} %get-tuple-element.10, bf16[96,1024]{1,0:T(8,128)(2,1)S(1)} %get-tuple-element.9), kind=kOutput, calls=%fused_computation.13 | convolution fusion | flops 806191104 | bytes 9568256 | tf_op jit(solution)/shard_map/dot_general | solution.py:72
  21.6 2.5 copy.18
  24.1 12.8 %scatter_custom_fusion.1 = f32[96,2048]{0,1:T(8,128)} fusion(s32[2048]{0:T(1024)S(1)} %bitcast.70, f32[2048,96]{1,0:T(8,128)} %copy.18, f32[]{:T(128)} %constant.36.clone.1), kind=kCustom, calls=%fused_computation.29 | custom fusion | flops 196608 | bytes 786944 | tf_op jit(solution)/shard_map/scatter-add | solution.py:80
  36.9 1.3 convert_element_type.78
  38.3 1.9 collective-permute-start.1
  40.2 5.6 %collective-permute-done.1 = bf16[96,1024]{0,1:T(8,128)(2,1)S(1)} collective-permute-done((bf16[96,1024]{0,1:T(8,128)(2,1)S(1)}, bf16[96,1024]{0,1:T(8,128)(2,1)S(1)}, u32[]{:S(2)}, u32[]{:S(2)}) %collective-permute-start.1) | collective-permute-done | bytes 196640 | tf_op jit(solution)/shard_map/ppermute | solution.py:12
  46.7 1.5 collective-permute-start.2
  49.0 1.0 copy.20
  50.0 1.9 collective-permute-done.2
  51.9 1.8 subtract_convert_fusion
  53.7 1.5 collective-permute-start.3
  56.1 2.9 %collective-permute-done.3 = bf16[96,512]{0,1:T(8,128)(2,1)} collective-permute-done((bf16[96,512]{0,1:T(8,128)(2,1)}, bf16[96,512]{0,1:T(8,128)(2,1)}, u32[]{:S(2)}, u32[]{:S(2)}) %collective-permute-start.3) | collective-permute-done | bytes 98336 | tf_op jit(solution)/shard_map/ppermute | solution.py:12
  60.7 1.5 collective-permute-start.4
  63.0 13.3 %scatter_custom_fusion = f32[96,4096]{0,1:T(8,128)} fusion(s32[2048]{0:T(1024)} %bitcast.69, f32[2048,96]{1,0:T(8,128)} %copy.18, f32[]{:T(128)} %constant.36.clone.1), kind=kCustom, calls=%fused_computation.21 | custom fusion | flops 196608 | bytes 1573376 | tf_op jit(solution)/shard_map/scatter-add | solution.py:83
  76.3 1.9 broadcast_select_fusion.1
  78.1 3.9 %convolution_bitcast_fusion = f32[3072,96]{0,1:T(8,128)} fusion(bf16[1,512,3072]{2,1,0:T(8,128)(2,1)S(1)} %copy-done, bf16[1,2048,512]{2,1,0:T(8,128)(2,1)} %param.16, bf16[96,1024]{0,1:T(8,128)(2,1)} %get-tuple-element.8, bf16[96,1024]{0,1:T(8,128)(2,1)} %get-tuple-element.7), kind=kOutput, calls=%fused_computation.11 | convolution fusion | flops 504152064 | bytes 6815744 | tf_op jit(solution)/shard_map/dot_general | solution.py:91
  82.0 2.9 %copy.21 = f32[3072,96]{1,0:T(8,128)} copy(f32[3072,96]{0,1:T(8,128)} %convolution_bitcast_fusion) | data formatting | bytes 2359296 | tf_op jit(solution)/shard_map/dot_general | solution.py:91
  84.9 18.5 %scatter_fusion = f32[96,4096]{0,1:T(8,128)} fusion(f32[96,4096]{0,1:T(8,128)} %scatter_custom_fusion, s32[3072]{0:T(1024)S(1)} %bitcast.68, f32[3072,96]{1,0:T(8,128)} %copy.21), kind=kCustom, calls=%fused_computation.2 | custom fusion | flops 294912 | bytes 3551232 | tf_op jit(solution)/shard_map/scatter-add | solution.py:93
  103.4 4.2 %fusion.52 = (f32[48,4096]{0,1:T(8,128)S(1)}, f32[48,4096]{0,1:T(8,128)}) fusion(f32[96,4096]{0,1:T(8,128)} %scatter_fusion), kind=kLoop, calls=%fused_computation.59 | loop fusion | bytes 3145728 | tf_op jit(solution)/shard_map/slice | solution.py:135
  107.6 1.1 convert_element_type.88
  108.8 78.7 %all-reduce.3.cloned.1.call-done = bf16[48,4096]{0,1:T(8,128)(2,1)} async-done(((bf16[48,4096]{0,1:T(8,128)(2,1)}), bf16[48,4096]{0,1:T(8,128)(2,1)}) %all-reduce.3.cloned.1.call-update) | async-done | bytes 393232 | tf_op jit(solution)/shard_map/psum | solution.py:102
  187.5 3.4 %convert_bitcast_fusion = (bf16[1,48,512]{2,1,0:T(8,128)(2,1)S(1)}, bf16[48,512]{1,0:T(8,128)(2,1)S(1)}) fusion(f32[512]{0:T(512)S(1)} %bitcast.71, bf16[1,4096,512]{2,1,0:T(8,128)(2,1)} %param.18, bf16[48,4096]{0,1:T(8,128)(2,1)} %all-reduce.3.cloned.1.call-done), kind=kOutput, calls=%fused_computation.51 | convolution fusion | flops 201990144 | bytes 4687872 | tf_op jit(solution)/shard_map/dot_general | solution.py:104
  190.9 1.8 collective-permute-start.5
  192.7 3.1 %copy.25 = f32[48,4096]{1,0:T(8,128)} copy(f32[48,4096]{0,1:T(8,128)} %get-tuple-element.6) | data formatting | bytes 1572864
  195.8 1.6 fusion.47
  197.3 1.9 convert_element_type.96
  199.3 72.2 %all-reduce.5.cloned.1.call-done = bf16[48,4096]{1,0:T(8,128)(2,1)} async-done(((bf16[48,4096]{1,0:T(8,128)(2,1)}), bf16[48,4096]{1,0:T(8,128)(2,1)}) %all-reduce.5.cloned.1.call-update) | async-done | bytes 393232 | tf_op jit(solution)/shard_map/psum | solution.py:102
  271.5 3.1 %fusion.25 = bf16[1,48,512]{2,1,0:T(8,128)(2,1)S(1)} fusion(bf16[1,4096,512]{2,1,0:T(8,128)(2,1)} %param.18, bf16[48,4096]{1,0:T(8,128)(2,1)} %all-reduce.5.cloned.1.call-done), kind=kOutput, calls=%fused_computation.20 | convolution fusion | flops 201940992 | bytes 4636672 | tf_op jit(solution)/shard_map/dot_general | solution.py:104
  (28 shorter events, 5.9 us)
Async XLA Ops:
  6.5 71.6 %copy-start = (bf16[1,512,3072]{2,1,0:T(8,128)(2,1)S(1)}, bf16[1,512,3072]{2,1,0:T(8,128)(2,1)}, u32[]{:S(2)}) copy-start(bf16[1,512,3072]{2,1,0:T(8,128)(2,1)} %param.17) | copy-start | bytes 9437188
  6.5 180.9 %all-reduce.3.cloned.1.call-start = ((), (), s32[]{:S(2)}) async-start(), calls=%async_computation | async-start | bytes 2097152 | tf_op jit(solution)/shard_map/psum | solution.py:102
  6.5 8.2 %collective-permute-start = (bf16[96,1024]{1,0:T(8,128)(2,1)}, bf16[96,1024]{1,0:T(8,128)(2,1)}, u32[]{:S(2)}, u32[]{:S(2)}) collective-permute-start(bf16[96,1024]{1,0:T(8,128)(2,1)} %bitcast.67), channel_id=1, source_target_pairs={{0,1},{1,0},{2,3},{3,2},{4,5},{5,4},{6,7},{7,6},{8,9},{9,8},{10,11... | collective-permute-start | bytes 589832 | tf_op jit(solution)/shard_map/ppermute | solution.py:12
  38.2 10.1 %copy-start.3 = (bf16[1,2,48,512]{3,2,1,0:T(8,128)(2,1)S(1)}, bf16[1,2,48,512]{3,2,1,0:T(8,128)(2,1)}, u32[]{:S(2)}) copy-start(bf16[1,2,48,512]{3,2,1,0:T(8,128)(2,1)} %param.12) | copy-start | bytes 294916
  38.3 7.5 %collective-permute-start.1 = (bf16[96,1024]{0,1:T(8,128)(2,1)S(1)}, bf16[96,1024]{0,1:T(8,128)(2,1)S(1)}, u32[]{:S(2)}, u32[]{:S(2)}) collective-permute-start(bf16[96,1024]{0,1:T(8,128)(2,1)S(1)} %select_convert_fusion), channel_id=1, source_target_pairs={{0,2},{1,3},{2,0},{3,1},{4,6},{5,7},{6,4},{7,5},{8,10},{9,11},{10,... | collective-permute-start | bytes 589832 | tf_op jit(solution)/shard_map/ppermute | solution.py:12
  45.9 0.8 copy-start.1
  46.7 5.1 %collective-permute-start.2 = (bf16[96,512]{0,1:T(8,128)(2,1)S(1)}, bf16[96,512]{0,1:T(8,128)(2,1)}, u32[]{:S(2)}, u32[]{:S(2)}) collective-permute-start(bf16[96,512]{0,1:T(8,128)(2,1)S(1)} %select_convert_fusion.1), channel_id=1, source_target_pairs={{0,1},{1,0},{2,3},{3,2},{4,5},{5,4},{6,7},{7,6},{8,9},{9,8},{10,11... | collective-permute-start | bytes 294920 | tf_op jit(solution)/shard_map/ppermute | solution.py:12
  53.7 5.3 %collective-permute-start.3 = (bf16[96,512]{0,1:T(8,128)(2,1)}, bf16[96,512]{0,1:T(8,128)(2,1)}, u32[]{:S(2)}, u32[]{:S(2)}) collective-permute-start(bf16[96,512]{0,1:T(8,128)(2,1)} %subtract_convert_fusion), channel_id=1, source_target_pairs={{0,1},{1,0},{2,3},{3,2},{4,5},{5,4},{6,7},{7,6},{8,9},{9,8},{10,11... | collective-permute-start | bytes 294920 | tf_op jit(solution)/shard_map/ppermute | solution.py:12
  60.7 15.6 %collective-permute-start.4 = (bf16[96,1024]{0,1:T(8,128)(2,1)}, bf16[96,1024]{0,1:T(8,128)(2,1)}, u32[]{:S(2)}, u32[]{:S(2)}) collective-permute-start(bf16[96,1024]{0,1:T(8,128)(2,1)} %pad_maximum_fusion), channel_id=1, source_target_pairs={{0,2},{1,3},{2,0},{3,1},{4,6},{5,7},{6,4},{7,5},{8,10},{9,11},{10,... | collective-permute-start | bytes 589832 | tf_op jit(solution)/shard_map/ppermute | solution.py:12
  107.6 79.9 %copy-start.4 = (f32[1,512]{1,0:T(1,128)S(1)}, f32[1,512]{1,0:T(1,128)}, u32[]{:S(2)}) copy-start(f32[1,512]{1,0:T(1,128)} %param.19) | copy-start | bytes 6148
  108.7 162.7 %all-reduce.5.cloned.1.call-start = ((), (), s32[]{:S(2)}) async-start(), calls=%async_computation.1 | async-start | bytes 786432 | tf_op jit(solution)/shard_map/psum | solution.py:102
  190.9 4.9 %copy-start.2 = (bf16[1,2,48,512]{3,2,1,0:T(8,128)(2,1)S(1)}, bf16[1,2,48,512]{3,2,1,0:T(8,128)(2,1)}, u32[]{:S(2)}) copy-start(bf16[1,2,48,512]{3,2,1,0:T(8,128)(2,1)} %param.13) | copy-start | bytes 294916
  190.9 4.9 %collective-permute-start.5 = (bf16[48,512]{1,0:T(8,128)(2,1)S(1)}, bf16[48,512]{1,0:T(8,128)(2,1)S(1)}, u32[]{:S(2)}, u32[]{:S(2)}) collective-permute-start(bf16[48,512]{1,0:T(8,128)(2,1)S(1)} %get-tuple-element.14), channel_id=1, source_target_pairs={{0,8},{8,16},{16,24},{1,9},{9,17},{17,25},{2,10},{10,18},{18,26},{... | collective-permute-start | bytes 147464 | tf_op jit(solution)/shard_map/ppermute | solution.py:18
Sparse Core Ops, SparseCore 0:
  108.9 78.5 all-reduce.2
  199.4 72.0 all-reduce.4
where the time goes:
time: 283 us; the launch traced here: 282 us
  waiting for transfers between devices  165 us (58%)
  other arithmetic  60.6 us (21%)
  matrix products  16.2 us (6%)
  local copies, waits for them, and re-layouts  15.3 us (5%)
  between operations  13.5 us (5%)
  starting transfers between devices  11.3 us (4%)
    psum x2, waiting for transfers between devices, root_level(): lax.psum(root_total.astype(jnp.bfloat16), 'front').astype(jnp.float32)  151 us
    scatter-add x1, other arithmetic, lower_levels(): return root_terms.at[:, parent_targets].add(parent_terms)  18.5 us
    ppermute x5, waiting for transfers between devices, partner_2(): return lax.ppermute(value, axis, pairs)  14.2 us
    scatter-add x1, other arithmetic, lower_levels(): jnp.zeros((row_count, S0), jnp.float32).at[:, to_root]  13.3 us
    scatter-add x1, other arithmetic, lower_levels(): own_parent = jnp.zeros((row_count, parent_size), jnp.float32).at[:, to_pa...  12.8 us
    ppermute x5, starting transfers between devices, partner_2(): return lax.ppermute(value, axis, pairs)  9.41 us
    dot_general x2, matrix products, root_level(): jnp.dot(root_now, root_inverse, preferred_element_type=jnp.float32)  6.52 us
    dot_general x1, matrix products, lower_levels(): jnp.dot(child_solved, child_update, preferred_element_type=jnp.float32)  5.84 us
  transfers between devices with their start and end apart: 8, of which 6 were waited for; matrix products, arithmetic and copies ran while one was open for 7% of the time, Pallas kernels for 0%

commit v1 on v0

--- a/solution.py
+++ b/solution.py
@@ -2,6 +2,7 @@
 import jax.numpy as jnp
 from jax import lax
 from jax.sharding import PartitionSpec as P
+from jax.lax import all_gather
 
 S0 = 4096
 
@@ -99,7 +100,12 @@
     own_cols = lax.dynamic_slice_in_dim(root_terms, front_index * share_width, share_width, 1)
     own_cols = own_cols + incoming.astype(jnp.float32) - root_rhs.astype(jnp.float32)
     root_total = lax.dynamic_update_slice_in_dim(root_terms, own_cols, front_index * share_width, 1)
-    summed = lax.psum(root_total.astype(jnp.bfloat16), "front").astype(jnp.float32)
+
+    def lanes_map(m):
+        part_now = all_gather(m, "front").sum(axis=0)
+        return part_now
+
+    summed = lanes_map(root_total.astype(jnp.bfloat16)).astype(jnp.float32)
     root_now = (-summed).astype(jnp.bfloat16)
     root_solved = jnp.dot(root_now, root_inverse, preferred_element_type=jnp.float32)
     return (

time: 283 us -> 262 us (0.926)
  waiting for transfers between devices: 165 us -> 136 us
  other arithmetic: 60.6 us -> 66.4 us
  local copies, waits for them, and re-layouts: 15.3 us -> 18.2 us
    psum x2 -> x0, waiting for transfers between devices: 151 us -> none  [root_level(): lax.psum(root_total.astype(jnp.bfloat16), 'front').astype(jnp.float32)]
    all_gather x0 -> x2, waiting for transfers between devices: none -> 120 us  [lanes_map(): part_now = all_gather(m, 'front').sum(axis=0)]
    reduce_sum x0 -> x2, other arithmetic: none -> 4.76 us  [lanes_map(): part_now = all_gather(m, 'front').sum(axis=0)]
    unnamed x12 -> x16, local copies, waits for them, and re-layouts: 4 us -> 6.95 us
where the time goes in v1:
time: 262 us; the launch traced here: 261 us
  waiting for transfers between devices  136 us (52%)
  other arithmetic  66.4 us (25%)
  local copies, waits for them, and re-layouts  18.2 us (7%)
  matrix products  16.4 us (6%)
  between operations  13.5 us (5%)
  starting transfers between devices  10.9 us (4%)
    all_gather x2, waiting for transfers between devices, lanes_map(): part_now = all_gather(m, 'front').sum(axis=0)  120 us
    scatter-add x1, other arithmetic, lower_levels(): return root_terms.at[:, parent_targets].add(parent_terms)  18.5 us
    ppermute x5, waiting for transfers between devices, partner_2(): return lax.ppermute(value, axis, pairs)  15.5 us
    scatter-add x1, other arithmetic, lower_levels(): jnp.zeros((row_count, S0), jnp.float32).at[:, to_root]  13.2 us
    scatter-add x1, other arithmetic, lower_levels(): own_parent = jnp.zeros((row_count, parent_size), jnp.float32).at[:, to_pa...  12.8 us
    ppermute x5, starting transfers between devices, partner_2(): return lax.ppermute(value, axis, pairs)  9.47 us
    unnamed x16, local copies, waits for them, and re-layouts  6.95 us
    dot_general x2, matrix products, root_level(): jnp.dot(root_now, root_inverse, preferred_element_type=jnp.float32)  6.7 us
  transfers between devices with their start and end apart: 8, of which 6 were waited for; matrix products, arithmetic and copies ran while one was open for 7% of the time, Pallas kernels for 0%

profile of v1, /device:TPU:0, one launch (start us, length us, event | category | flops | bytes accessed | tf_op | source)
XLA Modules:
  0.0 261.5 jit_solution(10639645892304315236)
XLA Ops:
  6.5 3.0 %collective-permute-start = (bf16[96,1024]{1,0:T(8,128)(2,1)}, bf16[96,1024]{1,0:T(8,128)(2,1)}, u32[]{:S(2)}, u32[]{:S(2)}) collective-permute-start(bf16[96,1024]{1,0:T(8,128)(2,1)} %bitcast.71), channel_id=1, source_target_pairs={{0,1},{1,0},{2,3},{3,2},{4,5},{5,4},{6,7},{7,6},{8,9},{9,8},{10,11... | collective-permute-start | bytes 589832 | tf_op jit(solution)/shard_map/ppermute | solution.py:13
  10.3 4.4 %collective-permute-done = bf16[96,1024]{1,0:T(8,128)(2,1)} collective-permute-done((bf16[96,1024]{1,0:T(8,128)(2,1)}, bf16[96,1024]{1,0:T(8,128)(2,1)}, u32[]{:S(2)}, u32[]{:S(2)}) %collective-permute-start) | collective-permute-done | bytes 196640 | tf_op jit(solution)/shard_map/ppermute | solution.py:13
  15.8 5.8 %fusion.9 = f32[2048,96]{0,1:T(8,128)} fusion(bf16[1,1024,2048]{2,1,0:T(8,128)(2,1)} %param.15, bf16[1,2048,1024]{2,1,0:T(8,128)(2,1)} %param.14, bf16[96,1024]{1,0:T(8,128)(2,1)S(1)} %get-tuple-element.10, bf16[96,1024]{1,0:T(8,128)(2,1)S(1)} %get-tuple-element.9), kind=kOutput, calls=%fused_computation.13 | convolution fusion | flops 806191104 | bytes 9568256 | tf_op jit(solution)/shard_map/dot_general | solution.py:73
  21.6 2.5 copy.32
  24.1 12.8 %scatter_custom_fusion.1 = f32[96,2048]{0,1:T(8,128)} fusion(s32[2048]{0:T(1024)S(1)} %bitcast.74, f32[2048,96]{1,0:T(8,128)} %copy.32, f32[]{:T(128)} %constant.39.clone.1), kind=kCustom, calls=%fused_computation.29 | custom fusion | flops 196608 | bytes 786944 | tf_op jit(solution)/shard_map/scatter-add | solution.py:81
  36.9 1.3 convert_element_type.82
  38.3 1.9 collective-permute-start.1
  40.2 5.6 %collective-permute-done.1 = bf16[96,1024]{0,1:T(8,128)(2,1)S(1)} collective-permute-done((bf16[96,1024]{0,1:T(8,128)(2,1)S(1)}, bf16[96,1024]{0,1:T(8,128)(2,1)S(1)}, u32[]{:S(2)}, u32[]{:S(2)}) %collective-permute-start.1) | collective-permute-done | bytes 196640 | tf_op jit(solution)/shard_map/ppermute | solution.py:13
  46.7 1.5 collective-permute-start.2
  50.0 1.9 collective-permute-done.2
  53.0 1.5 collective-permute-start.3
  54.6 3.6 %collective-permute-done.3 = bf16[96,512]{0,1:T(8,128)(2,1)} collective-permute-done((bf16[96,512]{0,1:T(8,128)(2,1)S(1)}, bf16[96,512]{0,1:T(8,128)(2,1)}, u32[]{:S(2)}, u32[]{:S(2)}) %collective-permute-start.3) | collective-permute-done | bytes 98336 | tf_op jit(solution)/shard_map/ppermute | solution.py:13
  59.8 1.5 collective-permute-start.4
  62.2 13.2 %scatter_custom_fusion = f32[96,4096]{0,1:T(8,128)} fusion(s32[2048]{0:T(1024)S(1)} %bitcast.73, f32[2048,96]{1,0:T(8,128)} %copy.32, f32[]{:T(128)} %constant.39.clone.1), kind=kCustom, calls=%fused_computation.20 | custom fusion | flops 196608 | bytes 1573376 | tf_op jit(solution)/shard_map/scatter-add | solution.py:84
  75.4 1.9 broadcast_select_fusion.1
  77.3 3.9 %convolution_bitcast_fusion = f32[3072,96]{0,1:T(8,128)} fusion(bf16[1,512,3072]{2,1,0:T(8,128)(2,1)S(1)} %copy-done, bf16[1,2048,512]{2,1,0:T(8,128)(2,1)} %param.16, bf16[96,1024]{0,1:T(8,128)(2,1)} %get-tuple-element.8, bf16[96,1024]{0,1:T(8,128)(2,1)} %get-tuple-element.7), kind=kOutput, calls=%fused_computation.11 | convolution fusion | flops 504152064 | bytes 6815744 | tf_op jit(solution)/shard_map/dot_general | solution.py:92
  81.2 2.9 %copy.35 = f32[3072,96]{1,0:T(8,128)} copy(f32[3072,96]{0,1:T(8,128)} %convolution_bitcast_fusion) | data formatting | bytes 2359296 | tf_op jit(solution)/shard_map/dot_general | solution.py:92
  84.1 18.5 %scatter_fusion = f32[96,4096]{0,1:T(8,128)} fusion(f32[96,4096]{0,1:T(8,128)} %scatter_custom_fusion, s32[3072]{0:T(1024)S(1)} %bitcast.72, f32[3072,96]{1,0:T(8,128)} %copy.35), kind=kCustom, calls=%fused_computation.2 | custom fusion | flops 294912 | bytes 3551232 | tf_op jit(solution)/shard_map/scatter-add | solution.py:94
  102.6 4.8 %fusion.52 = (f32[48,4096]{0,1:T(8,128)}, f32[48,4096]{0,1:T(8,128)}) fusion(f32[96,4096]{0,1:T(8,128)} %scatter_fusion), kind=kLoop, calls=%fused_computation.59 | loop fusion | bytes 3145728 | tf_op jit(solution)/shard_map/slice | solution.py:141
  107.4 3.1 %copy.38 = f32[48,4096]{1,0:T(8,128)} copy(f32[48,4096]{0,1:T(8,128)} %get-tuple-element.5) | data formatting | bytes 1572864
  110.5 1.6 fusion.47
  112.0 2.0 convert_element_type.92
  114.1 60.4 %all-gather.5.cloned.1.call-done = bf16[384,4096]{1,0:T(8,128)(2,1)} async-done(((bf16[48,4096]{1,0:T(8,128)(2,1)}), bf16[384,4096]{1,0:T(8,128)(2,1)}) %all-gather.5.cloned.1.call-update) | async-done | bytes 3145744 | tf_op jit(solution)/shard_map/all_gather | solution.py:105
  174.4 2.4 reduce_sum.24
  176.8 3.7 %convert_bitcast_fusion = (bf16[1,48,512]{2,1,0:T(8,128)(2,1)}, bf16[48,512]{1,0:T(8,128)(2,1)}) fusion(f32[512]{0:T(512)S(1)} %bitcast.75, bf16[1,4096,512]{2,1,0:T(8,128)(2,1)} %param.18, bf16[48,4096]{1,0:T(8,128)(2,1)S(1)} %reduce_sum.24), kind=kOutput, calls=%fused_computation.51 | convolution fusion | flops 201990144 | bytes 4687872 | tf_op jit(solution)/shard_map/dot_general | solution.py:110
  180.5 1.4 collective-permute-start.5
  181.9 3.1 %copy.39 = f32[48,4096]{1,0:T(8,128)} copy(f32[48,4096]{0,1:T(8,128)} %get-tuple-element.6) | data formatting | bytes 1572864
  185.0 1.6 fusion.46
  186.5 1.9 convert_element_type.100
  188.5 60.1 %all-gather.7.cloned.1.call-done = bf16[384,4096]{1,0:T(8,128)(2,1)} async-done(((bf16[48,4096]{1,0:T(8,128)(2,1)}), bf16[384,4096]{1,0:T(8,128)(2,1)}) %all-gather.7.cloned.1.call-update) | async-done | bytes 3145744 | tf_op jit(solution)/shard_map/all_gather | solution.py:105
  248.6 2.4 reduce_sum.25
  251.0 3.0 %fusion.25 = bf16[1,48,512]{2,1,0:T(8,128)(2,1)S(1)} fusion(bf16[1,4096,512]{2,1,0:T(8,128)(2,1)} %param.18, bf16[48,4096]{1,0:T(8,128)(2,1)S(1)} %reduce_sum.25), kind=kOutput, calls=%fused_computation.19 | convolution fusion | flops 201940992 | bytes 4636672 | tf_op jit(solution)/shard_map/dot_general | solution.py:110
  (33 shorter events, 8.9 us)
Async XLA Ops:
  6.5 70.8 %copy-start = (bf16[1,512,3072]{2,1,0:T(8,128)(2,1)S(1)}, bf16[1,512,3072]{2,1,0:T(8,128)(2,1)}, u32[]{:S(2)}) copy-start(bf16[1,512,3072]{2,1,0:T(8,128)(2,1)} %param.17) | copy-start | bytes 9437188
  6.5 167.9 %all-gather.5.cloned.1.call-start = ((), (), s32[]{:S(2)}) async-start(), calls=%async_computation | async-start | bytes 3538944 | tf_op jit(solution)/shard_map/all_gather | solution.py:105
  6.5 8.2 %collective-permute-start = (bf16[96,1024]{1,0:T(8,128)(2,1)}, bf16[96,1024]{1,0:T(8,128)(2,1)}, u32[]{:S(2)}, u32[]{:S(2)}) collective-permute-start(bf16[96,1024]{1,0:T(8,128)(2,1)} %bitcast.71), channel_id=1, source_target_pairs={{0,1},{1,0},{2,3},{3,2},{4,5},{5,4},{6,7},{7,6},{8,9},{9,8},{10,11... | collective-permute-start | bytes 589832 | tf_op jit(solution)/shard_map/ppermute | solution.py:13
  38.2 10.1 %copy-start.3 = (bf16[1,2,48,512]{3,2,1,0:T(8,128)(2,1)S(1)}, bf16[1,2,48,512]{3,2,1,0:T(8,128)(2,1)}, u32[]{:S(2)}) copy-start(bf16[1,2,48,512]{3,2,1,0:T(8,128)(2,1)} %param.12) | copy-start | bytes 294916
  38.3 7.5 %collective-permute-start.1 = (bf16[96,1024]{0,1:T(8,128)(2,1)S(1)}, bf16[96,1024]{0,1:T(8,128)(2,1)S(1)}, u32[]{:S(2)}, u32[]{:S(2)}) collective-permute-start(bf16[96,1024]{0,1:T(8,128)(2,1)S(1)} %select_convert_fusion), channel_id=1, source_target_pairs={{0,2},{1,3},{2,0},{3,1},{4,6},{5,7},{6,4},{7,5},{8,10},{9,11},{10,... | collective-permute-start | bytes 589832 | tf_op jit(solution)/shard_map/ppermute | solution.py:13
  45.9 0.8 copy-start.1
  46.7 5.1 %collective-permute-start.2 = (bf16[96,512]{0,1:T(8,128)(2,1)S(1)}, bf16[96,512]{0,1:T(8,128)(2,1)}, u32[]{:S(2)}, u32[]{:S(2)}) collective-permute-start(bf16[96,512]{0,1:T(8,128)(2,1)S(1)} %select_convert_fusion.1), channel_id=1, source_target_pairs={{0,1},{1,0},{2,3},{3,2},{4,5},{5,4},{6,7},{7,6},{8,9},{9,8},{10,11... | collective-permute-start | bytes 294920 | tf_op jit(solution)/shard_map/ppermute | solution.py:13
  53.0 5.1 %collective-permute-start.3 = (bf16[96,512]{0,1:T(8,128)(2,1)S(1)}, bf16[96,512]{0,1:T(8,128)(2,1)}, u32[]{:S(2)}, u32[]{:S(2)}) collective-permute-start(bf16[96,512]{0,1:T(8,128)(2,1)S(1)} %subtract_convert_fusion), channel_id=1, source_target_pairs={{0,1},{1,0},{2,3},{3,2},{4,5},{5,4},{6,7},{7,6},{8,9},{9,8},{10,11... | collective-permute-start | bytes 294920 | tf_op jit(solution)/shard_map/ppermute | solution.py:13
  59.8 15.6 %collective-permute-start.4 = (bf16[96,1024]{0,1:T(8,128)(2,1)}, bf16[96,1024]{0,1:T(8,128)(2,1)}, u32[]{:S(2)}, u32[]{:S(2)}) collective-permute-start(bf16[96,1024]{0,1:T(8,128)(2,1)} %pad_maximum_fusion), channel_id=1, source_target_pairs={{0,2},{1,3},{2,0},{3,1},{4,6},{5,7},{6,4},{7,5},{8,10},{9,11},{10,... | collective-permute-start | bytes 589832 | tf_op jit(solution)/shard_map/ppermute | solution.py:13
  107.4 3.1 %copy-start.4 = (bf16[1,2,48,512]{3,2,1,0:T(8,128)(2,1)S(1)}, bf16[1,2,48,512]{3,2,1,0:T(8,128)(2,1)}, u32[]{:S(2)}) copy-start(bf16[1,2,48,512]{3,2,1,0:T(8,128)(2,1)} %param.13) | copy-start | bytes 294916
  114.0 62.8 %copy-start.6 = (f32[1,512]{1,0:T(1,128)S(1)}, f32[1,512]{1,0:T(1,128)}, u32[]{:S(2)}) copy-start(f32[1,512]{1,0:T(1,128)} %param.19) | copy-start | bytes 6148
  114.0 134.5 %all-gather.7.cloned.1.call-start = ((), (), s32[]{:S(2)}) async-start(), calls=%async_computation.1 | async-start | bytes 3538944 | tf_op jit(solution)/shard_map/all_gather | solution.py:105
  180.5 4.5 %copy-start.5 = (bf16[1,2,48,512]{3,2,1,0:T(8,128)(2,1)S(1)}, bf16[1,2,48,512]{3,2,1,0:T(8,128)(2,1)}, u32[]{:S(2)}) copy-start(bf16[1,2,48,512]{3,2,1,0:T(8,128)(2,1)} %param.13) | copy-start | bytes 294916
  180.5 4.5 %collective-permute-start.5 = (bf16[48,512]{1,0:T(8,128)(2,1)}, bf16[48,512]{1,0:T(8,128)(2,1)S(1)}, u32[]{:S(2)}, u32[]{:S(2)}) collective-permute-start(bf16[48,512]{1,0:T(8,128)(2,1)} %get-tuple-element.14), channel_id=1, source_target_pairs={{0,8},{8,16},{16,24},{1,9},{9,17},{17,25},{2,10},{10,18},{18,26},{... | collective-permute-start | bytes 147464 | tf_op jit(solution)/shard_map/ppermute | solution.py:19
  250.9 3.0 %copy-start.2 = (bf16[1,48,512]{2,1,0:T(8,128)(2,1)S(1)}, bf16[1,48,512]{2,1,0:T(8,128)(2,1)}, u32[]{:S(2)}) copy-start(bf16[1,48,512]{2,1,0:T(8,128)(2,1)} %get-tuple-element.13) | copy-start | bytes 147460
Sparse Core Ops, SparseCore 0:
  114.1 60.2 all-gather.4
  188.6 59.9 all-gather.6
